TPU v7x, 32 devices: a whole 2x2x4 slice. The times are simulated.
32 devices in a mesh: groups: 2 (over y), tm: 4 (over x, core), win: 4 (over z).
Axes of the slice: x: 2, y: 2, z: 4, core: 2. Of those that a mesh axis runs over, the one named last changes fastest.
Arguments:
- unitaries: float32 [8, 4, 2, 2, 256, 256], P(('groups', 'win'), 'tm'), parts along dimension 0, may hold values from -1 to 1, as said below
Outputs:
- propagators: float32 [8, 4, 2, 2, 256, 256], P(('groups', 'win'), 'tm'), parts along dimension 0
There are 2 independent parts, one for each index of `groups`. A program takes and returns all parts, laid end to end along the dimension named above; each array names one. Nothing has to cross between parts.
Inputs may be any that keep to these rules, and one draw needn't show every extreme that they name: `unitaries`: each slot's complex matrix is unitary.
All inputs are finite; a program needn't handle non-finite values.
Results may differ from a plain program's by a relative error of at most 0.0003.
Values sent between devices are 32-bit elements; how exact they have to be, the bound alone decides.
A program may use at most 64 MiB of HBM per device.

v0:
```python
import jax
import jax.numpy as jnp
from jax import lax
from jax.sharding import PartitionSpec as P


def prefix(value, axis, join, neutral):
    count, mine = (lax.axis_size(axis), lax.axis_index(axis))
    pieces = lax.all_gather(value, axis)
    running = jnp.full_like(value, 0) + jnp.asarray(neutral, value.dtype)

    def hop(position, running):
        longer = join(running, pieces[position])
        return jnp.where(position < mine, longer, running)

    return lax.fori_loop(0, count - 1, hop, running)


def from_root(value, axis, source):
    kept = jnp.where(lax.axis_index(axis) == source, value, 0).astype(value.dtype)
    return lax.psum(kept, axis)


def complex_product(left, right):
    hi = lax.Precision.HIGHEST
    real_part = jnp.dot(
        left[0], right[0], precision=hi, preferred_element_type=jnp.float32
    ) - jnp.dot(left[1], right[1], precision=hi, preferred_element_type=jnp.float32)
    imag_part = jnp.dot(
        left[0], right[1], precision=hi, preferred_element_type=jnp.float32
    ) + jnp.dot(left[1], right[0], precision=hi, preferred_element_type=jnp.float32)
    return jnp.stack([real_part, imag_part])


def later_first(earlier, later):
    return complex_product(later, earlier)


def on_device(unitaries):
    own_slots = unitaries[0, 0]
    width = own_slots.shape[-1]
    identity_pair = jnp.stack(
        [jnp.eye(width, dtype=jnp.float32), jnp.zeros((width, width), jnp.float32)]
    )
    prefixes = [own_slots[0]]
    prefixes.append(complex_product(own_slots[1], prefixes[-1]))
    block_total = prefixes[-1]
    before = prefix(block_total, "tm", later_first, identity_pair)
    through = complex_product(block_total, before)
    window_product = from_root(through, "tm", lax.axis_size("tm") - 1)
    window_carry = prefix(window_product, "win", later_first, identity_pair)
    offset = complex_product(before, window_carry)
    results = jnp.stack([complex_product(piece, offset) for piece in prefixes])
    return results[None, None]


def solution(mesh):
    placed = (P(("groups", "win"), "tm", None, None, None, None),)
    return jax.shard_map(
        on_device,
        mesh=mesh,
        in_specs=placed,
        out_specs=P(("groups", "win"), "tm", None, None, None, None),
        check_vma=False,
    )
```

profile of v0, /device:TPU:0, one launch (start us, length us, event | category | flops | bytes accessed | tf_op | source)
XLA Modules:
  0.0 168.4 jit_solution(17108181392384072371)
XLA Ops:
  6.5 1.5 fusion.67
  8.0 1.4 fusion.57
  9.5 1.4 convolution_subtract_fusion.6
  10.9 0.4 convolution_add_fusion.6
  11.3 0.8 pad_maximum_fusion
  12.3 25.3 %all-gather.6.cloned.1.call-done = f32[8,256,256]{2,1,0:T(8,128)} async-done(((f32[2,256,256]{2,1,0:T(8,128)}), f32[8,256,256]{2,1,0:T(8,128)}) %all-gather.6.cloned.1.call-update) | async-done | bytes 2097168 | tf_op jit(solution)/shard_map/all_gather | solution.py:9
  37.6 16.6 %while.26 = (s32[]{:T(128)}, f32[2,256,256]{2,1,0:T(8,128)S(1)}, s32[]{:T(128)}, f32[4,2,256,256]{3,2,1,0:T(8,128)}, s32[]{:T(128)}, /*index=5*/s32[]{:T(128)}, s32[]{}) while((s32[]{:T(128)}, f32[2,256,256]{2,1,0:T(8,128)S(1)}, s32[]{:T(128)}, f32[4,2,256,256]{3,2,1,0:T(8,128)}, s32[]{:T(128)}, /*index=5*/s32[]{:T(128)}, s32[]{}) %tuple.64), condition=%wide.region_1.2_spmd, body=%wide.region_0.1_spmd.sunk | while | flops 805699584 | bytes 5245035 | solution.py:16
  37.6 1.3 fusion.133
  38.9 1.3 fusion.134
  40.2 1.3 fusion.135
  41.6 1.3 fusion.136
  43.1 1.3 fusion.133
  44.4 1.3 fusion.134
  45.8 1.3 fusion.135
  47.1 1.3 fusion.136
  48.6 1.3 fusion.133
  49.9 1.3 fusion.134
  51.3 1.3 fusion.135
  52.6 1.3 fusion.136
  54.1 0.4 fusion.53
  54.5 0.4 fusion.47
  55.7 0.8 fusion.38
  56.8 33.1 %all-reduce.3.cloned.1.call-done = f32[1,2,256,256]{3,2,1,0:T(8,128)} async-done(((f32[1,2,256,256]{3,2,1,0:T(8,128)}), f32[1,2,256,256]{3,2,1,0:T(8,128)}) %all-reduce.3.cloned.1.call-update) | async-done | bytes 524304 | tf_op jit(solution)/shard_map/psum | solution.py:21
  89.9 47.5 %all-gather.4.cloned.1.call-done = f32[4,2,256,256]{3,2,1,0:T(8,128)} async-done(((f32[1,2,256,256]{3,2,1,0:T(8,128)}), f32[4,2,256,256]{3,2,1,0:T(8,128)}) %all-gather.4.cloned.1.call-update) | async-done | bytes 2097168 | tf_op jit(solution)/shard_map/all_gather | solution.py:9
  137.4 16.6 %while.27 = (s32[]{:T(128)}, f32[2,256,256]{2,1,0:T(8,128)S(1)}, s32[]{:T(128)}, f32[4,2,256,256]{3,2,1,0:T(8,128)}, s32[]{:T(128)}, /*index=5*/s32[]{:T(128)}, s32[]{}) while((s32[]{:T(128)}, f32[2,256,256]{2,1,0:T(8,128)S(1)}, s32[]{:T(128)}, f32[4,2,256,256]{3,2,1,0:T(8,128)}, s32[]{:T(128)}, /*index=5*/s32[]{:T(128)}, s32[]{}) %tuple.55), condition=%wide.region_4.5_spmd, body=%wide.region_3.4_spmd.sunk | while | flops 805699584 | bytes 5245035 | solution.py:16
  137.4 1.3 fusion.141
  138.8 1.3 fusion.142
  140.1 1.3 fusion.143
  141.4 1.3 fusion.144
  142.9 1.3 fusion.141
  144.3 1.3 fusion.142
  145.6 1.3 fusion.143
  147.0 1.3 fusion.144
  148.5 1.3 fusion.141
  149.8 1.3 fusion.142
  151.1 1.3 fusion.143
  152.5 1.3 fusion.144
  154.8 0.4 convolution_subtract_fusion.4
  155.2 0.6 fusion.95
  155.8 0.6 fusion.64
  156.4 0.4 convolution_add_fusion.4
  156.7 0.6 fusion.96
  157.4 0.6 fusion.62
  158.0 0.6 fusion.33
  158.6 0.6 fusion.32
  159.2 0.6 fusion.35
  159.8 0.6 fusion.34
  160.6 1.3 copy.11
  (23 shorter events, 2.9 us)
Async XLA Ops:
  6.5 4.3 %copy-start = (f32[1,1,2,2,256,256]{5,4,3,2,1,0:T(8,128)S(1)}, f32[1,1,2,2,256,256]{5,4,3,2,1,0:T(8,128)}, u32[]{:S(2)}) copy-start(f32[1,1,2,2,256,256]{5,4,3,2,1,0:T(8,128)} %param.5) | copy-start | bytes 3145732
  6.5 31.0 %all-gather.6.cloned.1.call-start = ((), (), s32[]{:S(2)}) async-start(), calls=%async_computation.2 | async-start | bytes 2621440 | tf_op jit(solution)/shard_map/all_gather | solution.py:9
  12.1 77.7 %all-reduce.3.cloned.1.call-start = ((), (), s32[]{:S(2)}) async-start(), calls=%async_computation | async-start | bytes 1048576 | tf_op jit(solution)/shard_map/psum | solution.py:21
  56.5 80.9 %all-gather.4.cloned.1.call-start = ((), (), s32[]{:S(2)}) async-start(), calls=%async_computation.1 | async-start | bytes 2621440 | tf_op jit(solution)/shard_map/all_gather | solution.py:9
Sparse Core Ops, SparseCore 0:
  12.3 25.2 all-gather.5
  56.7 33.1 all-reduce.2
  91.4 45.9 all-gather.3
where the time goes:
time: 169 us; the launch traced here: 168 us
  waiting for transfers between devices  106 us (63%)
  matrix products  44.5 us (26%)
  between operations  13.3 us (8%)
  other arithmetic  2.66 us (2%)
    all_gather x2, waiting for transfers between devices, prefix(): pieces = lax.all_gather(value, axis)  72.8 us
    psum x1, waiting for transfers between devices, from_root(): return lax.psum(kept, axis)  33.1 us
    dot_general x11, matrix products, complex_product(): jnp.dot(left[0], right[0], precision=hi, preferred_element_type=jnp.float32)  11.5 us
    dot_general x11, matrix products, complex_product(): jnp.dot(left[1], right[1], precision=hi, preferred_element_type=jnp.float32)  11.4 us
    dot_general x11, matrix products, complex_product(): jnp.dot(left[0], right[1], precision=hi, preferred_element_type=jnp.float32)  11.3 us
    dot_general x11, matrix products, complex_product(): jnp.dot(left[1], right[0], precision=hi, preferred_element_type=jnp.float32)  10.4 us
  transfers between devices with their start and end apart: 3, of which 3 were waited for; matrix products, arithmetic and copies ran while one was open for 0% of the time, Pallas kernels for 0%

commit v1 on v0

--- a/solution.py
+++ b/solution.py
@@ -2,6 +2,12 @@
 import jax.numpy as jnp
 from jax import lax
 from jax.sharding import PartitionSpec as P
+
+
+def summed_here(x, mesh_axis):
+    shards = lax.all_gather(x, mesh_axis, axis=0, tiled=False)
+    total = shards.sum(axis=0)
+    return total
 
 
 def prefix(value, axis, join, neutral):
@@ -18,7 +24,7 @@
 
 def from_root(value, axis, source):
     kept = jnp.where(lax.axis_index(axis) == source, value, 0).astype(value.dtype)
-    return lax.psum(kept, axis)
+    return summed_here(kept, axis)
 
 
 def complex_product(left, right):

time: 169 us -> 160 us (0.947)
  waiting for transfers between devices: 106 us -> 93.9 us
  other arithmetic: 2.66 us -> 5.24 us
    psum x1 -> x0, waiting for transfers between devices: 33.1 us -> none  [from_root(): return lax.psum(kept, axis)]
    all_gather x0 -> x1, waiting for transfers between devices: none -> 22.5 us  [summed_here(): shards = lax.all_gather(x, mesh_axis, axis=0, tiled=False)]
    reduce_sum x0 -> x1, other arithmetic: none -> 2.58 us  [summed_here(): total = shards.sum(axis=0)]
where the time goes in v1:
time: 160 us; the launch traced here: 159 us
  waiting for transfers between devices  93.9 us (59%)
  matrix products  44.5 us (28%)
  between operations  13.3 us (8%)
  other arithmetic  5.24 us (3%)
    all_gather x2, waiting for transfers between devices, prefix(): pieces = lax.all_gather(value, axis)  71.4 us
    all_gather x1, waiting for transfers between devices, summed_here(): shards = lax.all_gather(x, mesh_axis, axis=0, tiled=False)  22.5 us
    dot_general x11, matrix products, complex_product(): jnp.dot(left[0], right[0], precision=hi, preferred_element_type=jnp.float32)  11.4 us
    dot_general x11, matrix products, complex_product(): jnp.dot(left[1], right[1], precision=hi, preferred_element_type=jnp.float32)  11.4 us
    dot_general x11, matrix products, complex_product(): jnp.dot(left[0], right[1], precision=hi, preferred_element_type=jnp.float32)  11.3 us
    dot_general x11, matrix products, complex_product(): jnp.dot(left[1], right[0], precision=hi, preferred_element_type=jnp.float32)  10.4 us
  transfers between devices with their start and end apart: 3, of which 3 were waited for; matrix products, arithmetic and copies ran while one was open for 0% of the time, Pallas kernels for 0%

profile of v1, /device:TPU:0, one launch (start us, length us, event | category | flops | bytes accessed | tf_op | source)
XLA Modules:
  0.0 159.0 jit_solution(1830578403473986447)
XLA Ops:
  6.5 1.5 fusion.66
  8.0 1.4 fusion.56
  9.5 1.4 convolution_subtract_fusion.6
  10.9 0.4 convolution_add_fusion.6
  11.3 0.8 pad_maximum_fusion
  12.3 25.3 %all-gather.8.cloned.1.call-done = f32[8,256,256]{2,1,0:T(8,128)} async-done(((f32[2,256,256]{2,1,0:T(8,128)}), f32[8,256,256]{2,1,0:T(8,128)}) %all-gather.8.cloned.1.call-update) | async-done | bytes 2097168 | tf_op jit(solution)/shard_map/all_gather | solution.py:15
  37.6 16.6 %while.26 = (s32[]{:T(128)}, f32[2,256,256]{2,1,0:T(8,128)S(1)}, s32[]{:T(128)}, f32[4,2,256,256]{3,2,1,0:T(8,128)}, s32[]{:T(128)}, /*index=5*/s32[]{:T(128)}, s32[]{}) while((s32[]{:T(128)}, f32[2,256,256]{2,1,0:T(8,128)S(1)}, s32[]{:T(128)}, f32[4,2,256,256]{3,2,1,0:T(8,128)}, s32[]{:T(128)}, /*index=5*/s32[]{:T(128)}, s32[]{}) %tuple.64), condition=%wide.region_1.2_spmd, body=%wide.region_0.1_spmd.sunk | while | flops 805699584 | bytes 5245035 | solution.py:22
  37.6 1.3 fusion.132
  38.9 1.3 fusion.133
  40.2 1.3 fusion.134
  41.6 1.3 fusion.135
  43.1 1.3 fusion.132
  44.4 1.3 fusion.133
  45.8 1.3 fusion.134
  47.1 1.3 fusion.135
  48.6 1.3 fusion.132
  50.0 1.3 fusion.133
  51.3 1.3 fusion.134
  52.6 1.3 fusion.135
  55.3 0.4 fusion.36
  55.7 0.8 maximum_select_fusion.2
  56.8 22.5 %all-gather.6.cloned.1.call-done = f32[4,2,256,256]{3,2,1,0:T(8,128)} async-done(((f32[1,2,256,256]{3,2,1,0:T(8,128)}), f32[4,2,256,256]{3,2,1,0:T(8,128)}) %all-gather.6.cloned.1.call-update) | async-done | bytes 2097168 | tf_op jit(solution)/shard_map/all_gather | solution.py:8
  79.3 2.6 %reduce_sum.9 = f32[2,256,256]{2,1,0:T(8,128)} reduce(f32[4,2,256,256]{3,2,1,0:T(8,128)} %all-gather.6.cloned.1.call-done, f32[]{:T(128)} %constant.60.clone.1), dimensions={0}, to_apply=%region_2.3 | reduce | flops 393216 | bytes 2621444 | tf_op jit(solution)/shard_map/reduce_sum | solution.py:9
  81.9 46.1 %all-gather.10.cloned.1.call-done = f32[8,256,256]{2,1,0:T(8,128)} async-done(((f32[2,256,256]{2,1,0:T(8,128)}), f32[8,256,256]{2,1,0:T(8,128)}) %all-gather.10.cloned.1.call-update) | async-done | bytes 2097168 | tf_op jit(solution)/shard_map/all_gather | solution.py:15
  128.0 16.6 %while.27 = (s32[]{:T(128)}, f32[2,256,256]{2,1,0:T(8,128)S(1)}, s32[]{:T(128)}, f32[4,2,256,256]{3,2,1,0:T(8,128)}, s32[]{:T(128)}, /*index=5*/s32[]{:T(128)}, s32[]{}) while((s32[]{:T(128)}, f32[2,256,256]{2,1,0:T(8,128)S(1)}, s32[]{:T(128)}, f32[4,2,256,256]{3,2,1,0:T(8,128)}, s32[]{:T(128)}, /*index=5*/s32[]{:T(128)}, s32[]{}) %tuple.65), condition=%wide.region_4.5_spmd, body=%wide.region_3.4_spmd.sunk | while | flops 805699584 | bytes 5245035 | solution.py:22
  128.0 1.3 fusion.140
  129.3 1.3 fusion.141
  130.7 1.3 fusion.142
  132.0 1.3 fusion.143
  133.5 1.3 fusion.140
  134.9 1.3 fusion.141
  136.2 1.3 fusion.142
  137.5 1.3 fusion.143
  139.0 1.3 fusion.140
  140.4 1.3 fusion.141
  141.7 1.3 fusion.142
  143.1 1.3 fusion.143
  145.3 0.4 convolution_subtract_fusion.4
  145.7 0.6 fusion.94
  146.3 0.6 fusion.63
  146.9 0.4 convolution_add_fusion.4
  147.3 0.6 fusion.95
  147.9 0.6 fusion.61
  148.5 0.6 fusion.33
  149.1 0.6 fusion.32
  149.7 0.6 fusion.35
  150.4 0.6 fusion.34
  151.1 1.3 copy.11
  (24 shorter events, 3.3 us)
Async XLA Ops:
  6.5 4.3 %copy-start = (f32[1,1,2,2,256,256]{5,4,3,2,1,0:T(8,128)S(1)}, f32[1,1,2,2,256,256]{5,4,3,2,1,0:T(8,128)}, u32[]{:S(2)}) copy-start(f32[1,1,2,2,256,256]{5,4,3,2,1,0:T(8,128)} %param.5) | copy-start | bytes 3145732
  6.5 31.0 %all-gather.8.cloned.1.call-start = ((), (), s32[]{:S(2)}) async-start(), calls=%async_computation.1 | async-start | bytes 2621440 | tf_op jit(solution)/shard_map/all_gather | solution.py:15
  12.1 67.2 %all-gather.6.cloned.1.call-start = ((), (), s32[]{:S(2)}) async-start(), calls=%async_computation | async-start | bytes 2621440 | tf_op jit(solution)/shard_map/all_gather | solution.py:8
  56.5 71.4 %all-gather.10.cloned.1.call-start = ((), (), s32[]{:S(2)}) async-start(), calls=%async_computation.2 | async-start | bytes 2621440 | tf_op jit(solution)/shard_map/all_gather | solution.py:15
Sparse Core Ops, SparseCore 0:
  12.3 25.2 all-gather.7
  56.7 22.5 all-gather.5
  82.0 45.9 all-gather.9
